TPU v7x, 128 devices: a whole 4x4x4 slice. The times are simulated.
128 devices in a mesh: lat: 8 (over x_lo, z), lon: 16 (over x_hi, y, core).
Axes of the slice: x: 4 (x_hi: 2, x_lo: 2; x = x_hi * 2 + x_lo), y: 4, z: 4, core: 2. Of those that a mesh axis runs over, the one named last changes fastest.
Arguments:
- features: bfloat16 [32, 1024, 2048], P(None, 'lat', 'lon'), may hold values from -6 to 6
- cotangent: bfloat16 [32, 1024, 2048], P(None, 'lat', 'lon'), may hold values from -6 to 6
- sea_mask: int32 [1024, 2048], P('lat', 'lon'), may hold values 0 or 1
- weights: bfloat16 [5, 32, 32], replicated, may hold values from -1 to 1
Outputs:
- feature_grad: bfloat16 [32, 1024, 2048], P(None, 'lat', 'lon')
- weight_grad: float32 [5, 32, 32], replicated
Inputs may be any that keep to these rules, and one draw needn't show every extreme that they name: `sea_mask`: 1 marks a sea cell, 0 a land cell.
All inputs are finite; a program needn't handle non-finite values. No bound on the sum of `sea_mask` on one device may be relied on, other than what follows from the above.
Results may differ from a plain program's by a relative error of at most 0.0069.
Values sent between devices are 32-bit elements; how exact they have to be, the bound alone decides.
A program may use at most 128 MiB of HBM per device.

v0:
```python
import math
import jax
import jax.numpy as jnp
from jax import lax
from jax.sharding import PartitionSpec as P

K = 4
NEIGHBOURS = ((0, -1), (0, 1), (-1, 0), (1, 0), (-1, 1), (1, -1))


def padded_2(cells, sides, width, closed):
    for axis, dim in sides:
        count = lax.axis_size(axis)
        ends = count if closed else count - 1
        head = lax.slice_in_dim(cells, 0, width, axis=dim)
        tail = lax.slice_in_dim(cells, cells.shape[dim] - width, cells.shape[dim], axis=dim)
        cells = jnp.concatenate(
            [
                lax.ppermute(tail, axis, [(i, (i + 1) % count) for i in range(ends)]),
                cells,
                lax.ppermute(head, axis, [((i + 1) % count, i) for i in range(ends)]),
            ],
            axis=dim,
        )
    return cells


def neigh_sum(padded, outer_pad, inner_pad):
    row_count = padded.shape[-2] - 2 * (outer_pad - inner_pad)
    col_count = padded.shape[-1] - 2 * (outer_pad - inner_pad)
    base = outer_pad - inner_pad
    summed = None
    for step_row, step_col in NEIGHBOURS:
        shifted = padded[
            ...,
            base + step_row : base + step_row + row_count,
            base + step_col : base + step_col + col_count,
        ]
        summed = shifted if summed is None else summed + shifted
    return summed


def extend(cells_in, depth_cells):
    widened = padded_2(cells_in, (("lon", 2),), depth_cells, True)
    return padded_2(widened, (("lat", 1),), depth_cells, False)


def extend_flags(flag_cells, depth_cells):
    widened = padded_2(flag_cells, (("lon", 1),), depth_cells, True)
    return padded_2(widened, (("lat", 0),), depth_cells, False)


def local(features, cotangent, sea_mask, weights):
    flags_three = extend_flags(sea_mask, 3).astype(jnp.float32)
    degree = neigh_sum(flags_three, 3, 2)
    scale_two = flags_three[1:-1, 1:-1] / jnp.sqrt(jnp.maximum(degree, 1.0))
    scale_one = scale_two[1:-1, 1:-1]
    scale_zero = scale_two[2:-2, 2:-2]
    sea_cells = sea_mask.astype(jnp.float32)

    def laplace(cells_in):
        padded = extend(cells_in, 1)
        return -scale_zero * neigh_sum(scale_one * padded, 1, 0)

    initial = sea_cells * features.astype(jnp.float32)

    def keep_visit(carried, term):
        return carried + (term.astype(jnp.bfloat16),)

    carried = ()
    carried = keep_visit(carried, initial)
    previous = initial
    current = laplace(initial)
    carried = keep_visit(carried, current)
    for order_k in range(2, K + 1):
        advanced = 2.0 * laplace(current) - previous
        carried = keep_visit(carried, advanced)
        previous, current = (current, advanced)
    mixed = jnp.zeros(features.shape, jnp.float32)
    for index_k in range(K + 1):
        mixed = mixed + jnp.einsum(
            "cd,cij->dij", weights[index_k], carried[index_k], preferred_element_type=jnp.float32
        )
    activated = jnp.tanh(mixed)
    grad_mix = (cotangent.astype(jnp.float32) * (1.0 - activated * activated)).astype(jnp.bfloat16)
    weight_terms = jnp.stack(
        [
            jnp.einsum("cij,dij->cd", kept, grad_mix, preferred_element_type=jnp.float32)
            for kept in carried
        ]
    )
    summed = lax.psum(weight_terms, ("lat", "lon"))
    grid_cells = features.shape[1] * lax.axis_size("lat") * features.shape[2] * lax.axis_size("lon")
    weight_grad = summed * (1.0 / math.sqrt(grid_cells))

    def project(index_k):
        return jnp.einsum(
            "cd,dij->cij", weights[index_k], grad_mix, preferred_element_type=jnp.float32
        )

    upper_one = project(K)
    upper_two = jnp.zeros(features.shape, jnp.float32)
    for index_k in range(K - 1, 0, -1):
        fresh = project(index_k) + 2.0 * laplace(upper_one) - upper_two
        upper_two, upper_one = (upper_one, fresh)
    result = project(0) + laplace(upper_one) - upper_two
    feature_grad = (sea_cells * result).astype(jnp.bfloat16)
    return (feature_grad, weight_grad)


def solution(mesh):
    placed = (P(None, "lat", "lon"), P(None, "lat", "lon"), P("lat", "lon"), P())
    return jax.shard_map(
        local, mesh=mesh, in_specs=placed, out_specs=(P(None, "lat", "lon"), P()), check_vma=False
    )
```

profile of v0, /device:TPU:96, one launch (start us, length us, event | category | flops | bytes accessed | tf_op | source)
XLA Modules:
  0.0 407.8 jit_solution(406099193958542431)
XLA Ops:
  1.7 5.3 %collective-permute-start.1 = (s32[128,3]{1,0:T(8,128)S(1)}, s32[128,3]{1,0:T(8,128)S(1)}, u32[]{:S(2)}, u32[]{:S(2)}) collective-permute-start(s32[128,3]{1,0:T(8,128)S(1)} %get-tuple-element.41), channel_id=1, source_target_pairs={{1,0},{2,1},{3,2},{4,3},{5,4},{6,5},{7,6},{8,7},{9,8},{10,9},{11,1... | collective-permute-start | bytes 4616 | tf_op jit(solution)/shard_map/ppermute | solution.py:21
  12.0 3.8 collective-permute-start.3
  15.9 2.8 fusion.75
  21.3 2.7 copy.23
  24.0 5.4 %collective-permute-start.5 = (f32[32,128,1]{1,0,2:T(8,128)S(1)}, f32[32,128,1]{1,0,2:T(8,128)S(1)}, u32[]{:S(2)}, u32[]{:S(2)}) collective-permute-start(f32[32,128,1]{1,0,2:T(8,128)S(1)} %copy.23), channel_id=1, source_target_pairs={{1,0},{2,1},{3,2},{4,3},{5,4},{6,5},{7,6},{8,7},{9,8},{10,9},{11,1... | collective-permute-start | bytes 49160 | tf_op jit(solution)/shard_map/ppermute | solution.py:21
  29.8 2.9 copy.24
  32.7 2.8 copy.25
  36.5 4.3 %collective-permute-start.6 = (f32[32,1,130]{2,0,1:T(8,128)S(1)}, f32[32,1,130]{2,0,1:T(8,128)S(1)}, u32[]{:S(2)}, u32[]{:S(2)}) collective-permute-start(f32[32,1,130]{2,0,1:T(8,128)S(1)} %get-tuple-element.20), channel_id=1, source_target_pairs={{0,16},{16,32},{32,48},{48,64},{64,80},{80,96},{96,112},{1,17},{17... | collective-permute-start | bytes 49928 | tf_op jit(solution)/shard_map/ppermute | solution.py:19
  43.1 5.6 %collective-permute-done.7 = f32[32,1,130]{2,0,1:T(8,128)S(1)} collective-permute-done((f32[32,1,130]{2,0,1:T(8,128)S(1)}, f32[32,1,130]{2,0,1:T(8,128)S(1)}, u32[]{:S(2)}, u32[]{:S(2)}) %collective-permute-start.7) | collective-permute-done | bytes 16672 | tf_op jit(solution)/shard_map/ppermute | solution.py:21
  53.5 2.8 fusion.74
  58.9 2.7 copy.28
  61.6 5.4 %collective-permute-start.9 = (f32[32,128,1]{1,0,2:T(8,128)S(1)}, f32[32,128,1]{1,0,2:T(8,128)S(1)}, u32[]{:S(2)}, u32[]{:S(2)}) collective-permute-start(f32[32,128,1]{1,0,2:T(8,128)S(1)} %copy.28), channel_id=1, source_target_pairs={{1,0},{2,1},{3,2},{4,3},{5,4},{6,5},{7,6},{8,7},{9,8},{10,9},{11,1... | collective-permute-start | bytes 49160 | tf_op jit(solution)/shard_map/ppermute | solution.py:21
  67.0 2.9 copy.29
  69.9 2.9 copy.30
  75.9 4.3 %collective-permute-start.11 = (f32[32,1,130]{2,0,1:T(8,128)S(1)}, f32[32,1,130]{2,0,1:T(8,128)S(1)}, u32[]{:S(2)}, u32[]{:S(2)}) collective-permute-start(f32[32,1,130]{2,0,1:T(8,128)S(1)} %get-tuple-element.19), channel_id=1, source_target_pairs={{16,0},{32,16},{48,32},{64,48},{80,64},{96,80},{112,96},{17,1},{33... | collective-permute-start | bytes 49928 | tf_op jit(solution)/shard_map/ppermute | solution.py:21
  80.1 3.8 collective-permute-done.11
  86.4 4.1 %fusion.25 = f32[32,128,128]{2,0,1:T(8,128)S(1)} fusion(f32[32,130,130]{2,0,1:T(8,128)S(1)} %maximum_multiply_fusion.1, f32[128,128]{1,0:T(8,128)S(1)} %slice_negate_fusion, bf16[32,128,128]{2,1,0:T(8,128)(2,1)S(1)} %copy-done.33, f32[128,128]{1,0:T(8,128)S(1)} %convert_element_type.33), kind=kLoop, calls=%fused_computation.64 | loop fusion | flops 5242880 | bytes 15859712 | tf_op jit(solution)/shard_map/sub | solution.py:76
  90.5 2.8 fusion.73
  93.3 2.7 copy.32
  96.0 2.7 copy.33
  98.7 5.4 %collective-permute-start.13 = (f32[32,128,1]{1,0,2:T(8,128)S(1)}, f32[32,128,1]{1,0,2:T(8,128)S(1)}, u32[]{:S(2)}, u32[]{:S(2)}) collective-permute-start(f32[32,128,1]{1,0,2:T(8,128)S(1)} %copy.33), channel_id=1, source_target_pairs={{1,0},{2,1},{3,2},{4,3},{5,4},{6,5},{7,6},{8,7},{9,8},{10,9},{11,1... | collective-permute-start | bytes 49160 | tf_op jit(solution)/shard_map/ppermute | solution.py:21
  106.2 2.9 copy.34
  109.1 2.9 copy.35
  115.0 4.6 %collective-permute-start.15 = (f32[32,1,130]{2,0,1:T(8,128)S(1)}, f32[32,1,130]{2,0,1:T(8,128)S(1)}, u32[]{:S(2)}, u32[]{:S(2)}) collective-permute-start(f32[32,1,130]{2,0,1:T(8,128)S(1)} %get-tuple-element.17), channel_id=1, source_target_pairs={{16,0},{32,16},{48,32},{64,48},{80,64},{96,80},{112,96},{17,1},{33... | collective-permute-start | bytes 49928 | tf_op jit(solution)/shard_map/ppermute | solution.py:21
  123.1 3.9 maximum_multiply_fusion.2
  127.0 11.8 %fusion.22 = f32[32,128,128]{2,0,1:T(8,128)S(1)} fusion(f32[32,130,130]{2,0,1:T(8,128)} %maximum_multiply_fusion.2, f32[128,128]{1,0:T(8,128)S(1)} %slice_negate_fusion, f32[32,130,130]{2,0,1:T(8,128)S(1)} %bitcast.102), kind=kLoop, calls=%fused_computation.56 | loop fusion | flops 7340032 | bytes 27328512 | tf_op jit(solution)/shard_map/sub | solution.py:76
  138.8 2.8 fusion.72
  144.3 2.7 copy.38
  147.0 5.4 %collective-permute-start.17 = (f32[32,128,1]{1,0,2:T(8,128)S(1)}, f32[32,128,1]{1,0,2:T(8,128)S(1)}, u32[]{:S(2)}, u32[]{:S(2)}) collective-permute-start(f32[32,128,1]{1,0,2:T(8,128)S(1)} %copy.38), channel_id=1, source_target_pairs={{1,0},{2,1},{3,2},{4,3},{5,4},{6,5},{7,6},{8,7},{9,8},{10,9},{11,1... | collective-permute-start | bytes 49160 | tf_op jit(solution)/shard_map/ppermute | solution.py:21
  154.2 2.9 copy.39
  157.1 2.8 copy.40
  163.4 3.9 collective-permute-start.19
  171.5 3.8 maximum_multiply_fusion.3
  175.4 10.2 %fusion.19 = bf16[32,128,128]{2,0,1:T(8,128)(2,1)S(1)} fusion(f32[32,128,128]{2,0,1:T(8,128)S(1)} %fusion.25, f32[32,130,130]{2,0,1:T(8,128)} %maximum_multiply_fusion.3, f32[128,128]{1,0:T(8,128)S(1)} %slice_negate_fusion), kind=kLoop, calls=%fused_computation.48 | loop fusion | flops 4718592 | bytes 15794176 | tf_op jit(solution)/shard_map/convert_element_type | solution.py:68
  185.6 5.6 %fusion.27 = bf16[32,128,128]{2,0,1:T(8,128)(2,1)S(1)} fusion(f32[128,128,32]{1,2,0:T(8,128)} %fusion.34, f32[128,128,32]{1,2,0:T(8,128)} %fusion.37, f32[128,128,32]{1,2,0:T(8,128)} %fusion.43, f32[128,128,32]{1,2,0:T(8,128)} %fusion.40, bf16[32,128,128]{2,0,1:T(8,128)(2,1)S(1)} %fusion.19, bf16[32,128,128]{2,1,0:T(8,128)(2,1)} %param.5, ...), kind=kOutput, calls=%fused_computation.76 | convolution fusion | flops 38273024 | bytes 11542528 | tf_op jit(solution)/shard_map/cd,cij->dij/dot_general | solution.py:81
  191.6 2.9 fusion.71
  197.2 2.7 copy.48
  199.8 5.4 %collective-permute-start.21 = (f32[32,128,1]{1,0,2:T(8,128)S(1)}, f32[32,128,1]{1,0,2:T(8,128)S(1)}, u32[]{:S(2)}, u32[]{:S(2)}) collective-permute-start(f32[32,128,1]{1,0,2:T(8,128)S(1)} %copy.48), channel_id=1, source_target_pairs={{1,0},{2,1},{3,2},{4,3},{5,4},{6,5},{7,6},{8,7},{9,8},{10,9},{11,1... | collective-permute-start | bytes 49160 | tf_op jit(solution)/shard_map/ppermute | solution.py:21
  205.2 2.9 copy.49
  208.2 2.9 copy.50
  214.5 4.0 collective-permute-start.23
  218.4 3.9 collective-permute-done.23
  227.2 2.8 fusion.70
  232.7 2.7 copy.52
  235.3 5.4 %collective-permute-start.25 = (f32[32,128,1]{1,0,2:T(8,128)S(1)}, f32[32,128,1]{1,0,2:T(8,128)S(1)}, u32[]{:S(2)}, u32[]{:S(2)}) collective-permute-start(f32[32,128,1]{1,0,2:T(8,128)S(1)} %copy.52), channel_id=1, source_target_pairs={{1,0},{2,1},{3,2},{4,3},{5,4},{6,5},{7,6},{8,7},{9,8},{10,9},{11,1... | collective-permute-start | bytes 49160 | tf_op jit(solution)/shard_map/ppermute | solution.py:21
  240.7 2.7 fusion.32
  243.4 2.9 copy.53
  246.4 2.9 copy.54
  252.5 4.3 %collective-permute-start.27 = (f32[32,1,130]{2,0,1:T(8,128)S(1)}, f32[32,1,130]{2,0,1:T(8,128)S(1)}, u32[]{:S(2)}, u32[]{:S(2)}) collective-permute-start(f32[32,1,130]{2,0,1:T(8,128)S(1)} %get-tuple-element.11), channel_id=1, source_target_pairs={{16,0},{32,16},{48,32},{64,48},{80,64},{96,80},{112,96},{17,1},{33... | collective-permute-start | bytes 49928 | tf_op jit(solution)/shard_map/ppermute | solution.py:21
  265.3 2.7 fusion.69
  270.7 2.7 copy.56
  273.3 5.4 %collective-permute-start.29 = (f32[32,128,1]{1,0,2:T(8,128)S(1)}, f32[32,128,1]{1,0,2:T(8,128)S(1)}, u32[]{:S(2)}, u32[]{:S(2)}) collective-permute-start(f32[32,128,1]{1,0,2:T(8,128)S(1)} %copy.56), channel_id=1, source_target_pairs={{1,0},{2,1},{3,2},{4,3},{5,4},{6,5},{7,6},{8,7},{9,8},{10,9},{11,1... | collective-permute-start | bytes 49160 | tf_op jit(solution)/shard_map/ppermute | solution.py:21
  279.7 2.9 copy.57
  282.6 2.9 copy.58
  288.7 4.1 %collective-permute-start.31 = (f32[32,1,130]{2,0,1:T(8,128)S(1)}, f32[32,1,130]{2,0,1:T(8,128)S(1)}, u32[]{:S(2)}, u32[]{:S(2)}) collective-permute-start(f32[32,1,130]{2,0,1:T(8,128)S(1)} %get-tuple-element.9), channel_id=1, source_target_pairs={{16,0},{32,16},{48,32},{64,48},{80,64},{96,80},{112,96},{17,1},{33... | collective-permute-start | bytes 49928 | tf_op jit(solution)/shard_map/ppermute | solution.py:21
  293.9 2.8 collective-permute-done.31
  301.4 2.7 fusion.68
  306.9 3.2 copy.60
  310.1 5.3 %collective-permute-start.33 = (f32[32,128,1]{1,0,2:T(8,128)}, f32[32,128,1]{1,0,2:T(8,128)}, u32[]{:S(2)}, u32[]{:S(2)}) collective-permute-start(f32[32,128,1]{1,0,2:T(8,128)} %copy.60), channel_id=1, source_target_pairs={{1,0},{2,1},{3,2},{4,3},{5,4},{6,5},{7,6},{8,7},{9,8},{10,9},{11,1... | collective-permute-start | bytes 49160 | tf_op jit(solution)/shard_map/ppermute | solution.py:21
  317.7 62.9 %psum.7 = f32[5,32,32]{2,1,0:T(8,128)S(1)} all-reduce(f32[5,32,32]{2,1,0:T(8,128)} %fusion.28), channel_id=1, replica_groups=mesh['lat'=8,'lon'=16] {'lat','lon'}, use_global_device_ids=true, to_apply=%region_0.0 | all-reduce | flops 5120 | bytes 40960 | tf_op jit(solution)/shard_map/psum | solution.py:92
  380.7 3.6 copy.61
  384.3 3.6 copy.62
  388.9 4.4 %collective-permute-start.34 = (f32[32,1,130]{2,0,1:T(8,128)S(1)}, f32[32,1,130]{2,0,1:T(8,128)S(1)}, u32[]{:S(2)}, u32[]{:S(2)}) collective-permute-start(f32[32,1,130]{2,0,1:T(8,128)S(1)} %get-tuple-element.6), channel_id=1, source_target_pairs={{0,16},{16,32},{32,48},{48,64},{64,80},{80,96},{96,112},{1,17},{17... | collective-permute-start | bytes 49928 | tf_op jit(solution)/shard_map/ppermute | solution.py:19
  396.1 5.1 %collective-permute-done.35 = f32[32,1,130]{2,0,1:T(8,128)S(1)} collective-permute-done((f32[32,1,130]{2,0,1:T(8,128)S(1)}, f32[32,1,130]{2,0,1:T(8,128)S(1)}, u32[]{:S(2)}, u32[]{:S(2)}) %collective-permute-start.35) | collective-permute-done | bytes 16672 | tf_op jit(solution)/shard_map/ppermute | solution.py:21
  (173 shorter events, 99.6 us)
Async XLA Ops:
  0.6 9.3 %copy-start.35 = (s32[128,128]{1,0:T(8,128)S(1)}, s32[128,128]{1,0:T(8,128)}, u32[]{:S(2)}) copy-start(s32[128,128]{1,0:T(8,128)} %param.6) | copy-start | bytes 196612
  1.7 8.2 %collective-permute-start = (s32[128,3]{1,0:T(8,128)S(1)}, s32[128,3]{1,0:T(8,128)S(1)}, u32[]{:S(2)}, u32[]{:S(2)}) collective-permute-start(s32[128,3]{1,0:T(8,128)S(1)} %get-tuple-element.40), channel_id=1, source_target_pairs={{0,1},{1,2},{2,3},{3,4},{4,5},{5,6},{6,7},{7,8},{8,9},{9,10},{10,1... | collective-permute-start | bytes 4616 | tf_op jit(solution)/shard_map/ppermute | solution.py:19
  1.7 8.2 %collective-permute-start.1 = (s32[128,3]{1,0:T(8,128)S(1)}, s32[128,3]{1,0:T(8,128)S(1)}, u32[]{:S(2)}, u32[]{:S(2)}) collective-permute-start(s32[128,3]{1,0:T(8,128)S(1)} %get-tuple-element.41), channel_id=1, source_target_pairs={{1,0},{2,1},{3,2},{4,3},{5,4},{6,5},{7,6},{8,7},{9,8},{10,9},{11,1... | collective-permute-start | bytes 4616 | tf_op jit(solution)/shard_map/ppermute | solution.py:21
  10.0 19.4 %collective-permute-start.2 = (s32[3,134]{1,0:T(4,128)S(1)}, s32[3,134]{1,0:T(4,128)S(1)}, u32[]{:S(2)}, u32[]{:S(2)}) collective-permute-start(s32[3,134]{1,0:T(4,128)S(1)} %get-tuple-element.38), channel_id=1, source_target_pairs={{0,16},{16,32},{32,48},{48,64},{64,80},{80,96},{96,112},{1,17},{17... | collective-permute-start | bytes 4832 | tf_op jit(solution)/shard_map/ppermute | solution.py:19
  12.0 17.3 %collective-permute-start.3 = (s32[3,134]{1,0:T(4,128)S(1)}, s32[3,134]{1,0:T(4,128)S(1)}, u32[]{:S(2)}, u32[]{:S(2)}) collective-permute-start(s32[3,134]{1,0:T(4,128)S(1)} %get-tuple-element.39), channel_id=1, source_target_pairs={{16,0},{32,16},{48,32},{64,48},{80,64},{96,80},{112,96},{17,1},{33... | collective-permute-start | bytes 4832 | tf_op jit(solution)/shard_map/ppermute | solution.py:21
  21.3 8.5 %collective-permute-start.4 = (f32[32,128,1]{1,0,2:T(8,128)S(1)}, f32[32,128,1]{1,0,2:T(8,128)S(1)}, u32[]{:S(2)}, u32[]{:S(2)}) collective-permute-start(f32[32,128,1]{1,0,2:T(8,128)S(1)} %copy.22), channel_id=1, source_target_pairs={{0,1},{1,2},{2,3},{3,4},{4,5},{5,6},{6,7},{7,8},{8,9},{9,10},{10,1... | collective-permute-start | bytes 49160 | tf_op jit(solution)/shard_map/ppermute | solution.py:19
  24.0 8.7 %collective-permute-start.5 = (f32[32,128,1]{1,0,2:T(8,128)S(1)}, f32[32,128,1]{1,0,2:T(8,128)S(1)}, u32[]{:S(2)}, u32[]{:S(2)}) collective-permute-start(f32[32,128,1]{1,0,2:T(8,128)S(1)} %copy.23), channel_id=1, source_target_pairs={{1,0},{2,1},{3,2},{4,3},{5,4},{6,5},{7,6},{8,7},{9,8},{10,9},{11,1... | collective-permute-start | bytes 49160 | tf_op jit(solution)/shard_map/ppermute | solution.py:21
  35.5 13.2 %copy-start.17 = (f32[32,128,1]{2,0,1:T(8,128)S(1)}, f32[32,128,1]{2,0,1:T(8,128)}, u32[]{:S(2)}) copy-start(f32[32,128,1]{2,0,1:T(8,128)} %copy.24) | copy-start | bytes 49156
  35.5 13.2 %copy-start.25 = (f32[32,128,1]{2,0,1:T(8,128)S(1)}, f32[32,128,1]{2,0,1:T(8,128)}, u32[]{:S(2)}) copy-start(f32[32,128,1]{2,0,1:T(8,128)} %copy.25) | copy-start | bytes 49156
  36.5 6.6 %collective-permute-start.6 = (f32[32,1,130]{2,0,1:T(8,128)S(1)}, f32[32,1,130]{2,0,1:T(8,128)S(1)}, u32[]{:S(2)}, u32[]{:S(2)}) collective-permute-start(f32[32,1,130]{2,0,1:T(8,128)S(1)} %get-tuple-element.20), channel_id=1, source_target_pairs={{0,16},{16,32},{32,48},{48,64},{64,80},{80,96},{96,112},{1,17},{17... | collective-permute-start | bytes 49928 | tf_op jit(solution)/shard_map/ppermute | solution.py:19
  40.8 7.9 %collective-permute-start.7 = (f32[32,1,130]{2,0,1:T(8,128)S(1)}, f32[32,1,130]{2,0,1:T(8,128)S(1)}, u32[]{:S(2)}, u32[]{:S(2)}) collective-permute-start(f32[32,1,130]{2,0,1:T(8,128)S(1)} %get-tuple-element.21), channel_id=1, source_target_pairs={{16,0},{32,16},{48,32},{64,48},{80,64},{96,80},{112,96},{17,1},{33... | collective-permute-start | bytes 49928 | tf_op jit(solution)/shard_map/ppermute | solution.py:21
  53.5 30.4 %copy-start.1 = (f32[32,128,128]{2,0,1:T(8,128)}, f32[32,128,128]{2,0,1:T(8,128)S(1)}, u32[]{:S(2)}) copy-start(f32[32,128,128]{2,0,1:T(8,128)S(1)} %fusion.26) | copy-start | bytes 6291460
  58.9 8.1 %collective-permute-start.8 = (f32[32,128,1]{1,0,2:T(8,128)S(1)}, f32[32,128,1]{1,0,2:T(8,128)S(1)}, u32[]{:S(2)}, u32[]{:S(2)}) collective-permute-start(f32[32,128,1]{1,0,2:T(8,128)S(1)} %copy.27), channel_id=1, source_target_pairs={{0,1},{1,2},{2,3},{3,4},{4,5},{5,6},{6,7},{7,8},{8,9},{9,10},{10,1... | collective-permute-start | bytes 49160 | tf_op jit(solution)/shard_map/ppermute | solution.py:19
  61.6 8.3 %collective-permute-start.9 = (f32[32,128,1]{1,0,2:T(8,128)S(1)}, f32[32,128,1]{1,0,2:T(8,128)S(1)}, u32[]{:S(2)}, u32[]{:S(2)}) collective-permute-start(f32[32,128,1]{1,0,2:T(8,128)S(1)} %copy.28), channel_id=1, source_target_pairs={{1,0},{2,1},{3,2},{4,3},{5,4},{6,5},{7,6},{8,7},{9,8},{10,9},{11,1... | collective-permute-start | bytes 49160 | tf_op jit(solution)/shard_map/ppermute | solution.py:21
  72.8 11.1 %copy-start.23 = (f32[32,128,1]{2,0,1:T(8,128)S(1)}, f32[32,128,1]{2,0,1:T(8,128)}, u32[]{:S(2)}) copy-start(f32[32,128,1]{2,0,1:T(8,128)} %copy.29) | copy-start | bytes 49156
  72.8 11.1 %copy-start.31 = (f32[32,128,1]{2,0,1:T(8,128)S(1)}, f32[32,128,1]{2,0,1:T(8,128)}, u32[]{:S(2)}) copy-start(f32[32,128,1]{2,0,1:T(8,128)} %copy.30) | copy-start | bytes 49156
  73.8 6.3 %collective-permute-start.10 = (f32[32,1,130]{2,0,1:T(8,128)S(1)}, f32[32,1,130]{2,0,1:T(8,128)S(1)}, u32[]{:S(2)}, u32[]{:S(2)}) collective-permute-start(f32[32,1,130]{2,0,1:T(8,128)S(1)} %get-tuple-element.18), channel_id=1, source_target_pairs={{0,16},{16,32},{32,48},{48,64},{64,80},{80,96},{96,112},{1,17},{17... | collective-permute-start | bytes 49928 | tf_op jit(solution)/shard_map/ppermute | solution.py:19
  75.8 10.6 %copy-start.33 = (bf16[32,128,128]{2,1,0:T(8,128)(2,1)S(1)}, bf16[32,128,128]{2,1,0:T(8,128)(2,1)}, u32[]{:S(2)}) copy-start(bf16[32,128,128]{2,1,0:T(8,128)(2,1)} %param.4) | copy-start | bytes 3145732
  75.9 8.0 %collective-permute-start.11 = (f32[32,1,130]{2,0,1:T(8,128)S(1)}, f32[32,1,130]{2,0,1:T(8,128)S(1)}, u32[]{:S(2)}, u32[]{:S(2)}) collective-permute-start(f32[32,1,130]{2,0,1:T(8,128)S(1)} %get-tuple-element.19), channel_id=1, source_target_pairs={{16,0},{32,16},{48,32},{64,48},{80,64},{96,80},{112,96},{17,1},{33... | collective-permute-start | bytes 49928 | tf_op jit(solution)/shard_map/ppermute | solution.py:21
  93.3 10.8 %copy-start.36 = (bf16[5,32,32]{2,1,0:T(8,128)(2,1)S(1)}, bf16[5,32,32]{2,1,0:T(8,128)(2,1)}, u32[]{:S(2)}) copy-start(bf16[5,32,32]{2,1,0:T(8,128)(2,1)} %param.7) | copy-start | bytes 30724
  96.0 10.3 %collective-permute-start.12 = (f32[32,128,1]{1,0,2:T(8,128)S(1)}, f32[32,128,1]{1,0,2:T(8,128)S(1)}, u32[]{:S(2)}, u32[]{:S(2)}) collective-permute-start(f32[32,128,1]{1,0,2:T(8,128)S(1)} %copy.32), channel_id=1, source_target_pairs={{0,1},{1,2},{2,3},{3,4},{4,5},{5,6},{6,7},{7,8},{8,9},{9,10},{10,1... | collective-permute-start | bytes 49160 | tf_op jit(solution)/shard_map/ppermute | solution.py:19
  98.7 10.5 %collective-permute-start.13 = (f32[32,128,1]{1,0,2:T(8,128)S(1)}, f32[32,128,1]{1,0,2:T(8,128)S(1)}, u32[]{:S(2)}, u32[]{:S(2)}) collective-permute-start(f32[32,128,1]{1,0,2:T(8,128)S(1)} %copy.33), channel_id=1, source_target_pairs={{1,0},{2,1},{3,2},{4,3},{5,4},{6,5},{7,6},{8,7},{9,8},{10,9},{11,1... | collective-permute-start | bytes 49160 | tf_op jit(solution)/shard_map/ppermute | solution.py:21
  112.0 7.6 %copy-start.2 = (f32[32,128,128]{2,0,1:T(8,128)S(1)}, f32[32,128,128]{2,0,1:T(8,128)}, u32[]{:S(2)}) copy-start(f32[32,128,128]{2,0,1:T(8,128)} %copy-done.1) | copy-start | bytes 6291460
  113.0 8.4 %collective-permute-start.14 = (f32[32,1,130]{2,0,1:T(8,128)S(1)}, f32[32,1,130]{2,0,1:T(8,128)S(1)}, u32[]{:S(2)}, u32[]{:S(2)}) collective-permute-start(f32[32,1,130]{2,0,1:T(8,128)S(1)} %get-tuple-element.16), channel_id=1, source_target_pairs={{0,16},{16,32},{32,48},{48,64},{64,80},{80,96},{96,112},{1,17},{17... | collective-permute-start | bytes 49928 | tf_op jit(solution)/shard_map/ppermute | solution.py:19
  114.9 8.2 %copy-start.21 = (f32[32,128,1]{2,0,1:T(8,128)S(1)}, f32[32,128,1]{2,0,1:T(8,128)}, u32[]{:S(2)}) copy-start(f32[32,128,1]{2,0,1:T(8,128)} %copy.34) | copy-start | bytes 49156
  114.9 8.2 %copy-start.29 = (f32[32,128,1]{2,0,1:T(8,128)S(1)}, f32[32,128,1]{2,0,1:T(8,128)}, u32[]{:S(2)}) copy-start(f32[32,128,1]{2,0,1:T(8,128)} %copy.35) | copy-start | bytes 49156
  115.0 8.2 %collective-permute-start.15 = (f32[32,1,130]{2,0,1:T(8,128)S(1)}, f32[32,1,130]{2,0,1:T(8,128)S(1)}, u32[]{:S(2)}, u32[]{:S(2)}) collective-permute-start(f32[32,1,130]{2,0,1:T(8,128)S(1)} %get-tuple-element.17), channel_id=1, source_target_pairs={{16,0},{32,16},{48,32},{64,48},{80,64},{96,80},{112,96},{17,1},{33... | collective-permute-start | bytes 49928 | tf_op jit(solution)/shard_map/ppermute | solution.py:21
  119.6 7.4 %slice-start = ((s8[4259840]{0:T(1024)(128)(4,1)}), s8[4194304]{0:T(1024)(128)(4,1)S(1)}, s32[]{:S(2)}) async-start(s8[4259840]{0:T(1024)(128)(4,1)} %bitcast.101), calls=%async_computation | async-start | bytes 8388608
  144.3 9.9 %collective-permute-start.16 = (f32[32,128,1]{1,0,2:T(8,128)S(1)}, f32[32,128,1]{1,0,2:T(8,128)S(1)}, u32[]{:S(2)}, u32[]{:S(2)}) collective-permute-start(f32[32,128,1]{1,0,2:T(8,128)S(1)} %copy.37), channel_id=1, source_target_pairs={{0,1},{1,2},{2,3},{3,4},{4,5},{5,6},{6,7},{7,8},{8,9},{9,10},{10,1... | collective-permute-start | bytes 49160 | tf_op jit(solution)/shard_map/ppermute | solution.py:19
  147.0 10.1 %collective-permute-start.17 = (f32[32,128,1]{1,0,2:T(8,128)S(1)}, f32[32,128,1]{1,0,2:T(8,128)S(1)}, u32[]{:S(2)}, u32[]{:S(2)}) collective-permute-start(f32[32,128,1]{1,0,2:T(8,128)S(1)} %copy.38), channel_id=1, source_target_pairs={{1,0},{2,1},{3,2},{4,3},{5,4},{6,5},{7,6},{8,7},{9,8},{10,9},{11,1... | collective-permute-start | bytes 49160 | tf_op jit(solution)/shard_map/ppermute | solution.py:21
  159.9 7.4 %copy-start.5 = (f32[32,128,128]{2,0,1:T(8,128)S(1)}, f32[32,128,128]{2,0,1:T(8,128)}, u32[]{:S(2)}) copy-start(f32[32,128,128]{2,0,1:T(8,128)} %copy-done.4) | copy-start | bytes 6291460
  161.0 8.1 %collective-permute-start.18 = (f32[32,1,130]{2,0,1:T(8,128)S(1)}, f32[32,1,130]{2,0,1:T(8,128)S(1)}, u32[]{:S(2)}, u32[]{:S(2)}) collective-permute-start(f32[32,1,130]{2,0,1:T(8,128)S(1)} %get-tuple-element.14), channel_id=1, source_target_pairs={{0,16},{16,32},{32,48},{48,64},{64,80},{80,96},{96,112},{1,17},{17... | collective-permute-start | bytes 49928 | tf_op jit(solution)/shard_map/ppermute | solution.py:19
  163.3 8.2 %copy-start.22 = (f32[32,128,1]{2,0,1:T(8,128)S(1)}, f32[32,128,1]{2,0,1:T(8,128)}, u32[]{:S(2)}) copy-start(f32[32,128,1]{2,0,1:T(8,128)} %copy.39) | copy-start | bytes 49156
  163.3 8.2 %copy-start.30 = (f32[32,128,1]{2,0,1:T(8,128)S(1)}, f32[32,128,1]{2,0,1:T(8,128)}, u32[]{:S(2)}) copy-start(f32[32,128,1]{2,0,1:T(8,128)} %copy.40) | copy-start | bytes 49156
  163.4 8.2 %collective-permute-start.19 = (f32[32,1,130]{2,0,1:T(8,128)S(1)}, f32[32,1,130]{2,0,1:T(8,128)S(1)}, u32[]{:S(2)}, u32[]{:S(2)}) collective-permute-start(f32[32,1,130]{2,0,1:T(8,128)S(1)} %get-tuple-element.15), channel_id=1, source_target_pairs={{16,0},{32,16},{48,32},{64,48},{80,64},{96,80},{112,96},{17,1},{33... | collective-permute-start | bytes 49928 | tf_op jit(solution)/shard_map/ppermute | solution.py:21
  197.1 8.1 %collective-permute-start.20 = (f32[32,128,1]{1,0,2:T(8,128)S(1)}, f32[32,128,1]{1,0,2:T(8,128)S(1)}, u32[]{:S(2)}, u32[]{:S(2)}) collective-permute-start(f32[32,128,1]{1,0,2:T(8,128)S(1)} %copy.47), channel_id=1, source_target_pairs={{0,1},{1,2},{2,3},{3,4},{4,5},{5,6},{6,7},{7,8},{8,9},{9,10},{10,1... | collective-permute-start | bytes 49160 | tf_op jit(solution)/shard_map/ppermute | solution.py:19
  199.8 8.3 %collective-permute-start.21 = (f32[32,128,1]{1,0,2:T(8,128)S(1)}, f32[32,128,1]{1,0,2:T(8,128)S(1)}, u32[]{:S(2)}, u32[]{:S(2)}) collective-permute-start(f32[32,128,1]{1,0,2:T(8,128)S(1)} %copy.48), channel_id=1, source_target_pairs={{1,0},{2,1},{3,2},{4,3},{5,4},{6,5},{7,6},{8,7},{9,8},{10,9},{11,1... | collective-permute-start | bytes 49160 | tf_op jit(solution)/shard_map/ppermute | solution.py:21
  211.1 11.3 %copy-start.8 = (f32[32,128,128]{2,0,1:T(8,128)S(1)}, f32[32,128,128]{2,0,1:T(8,128)}, u32[]{:S(2)}) copy-start(f32[32,128,128]{2,0,1:T(8,128)} %copy-done.7) | copy-start | bytes 6291460
  211.1 11.3 %copy-start.24 = (f32[32,128,1]{2,0,1:T(8,128)S(1)}, f32[32,128,1]{2,0,1:T(8,128)}, u32[]{:S(2)}) copy-start(f32[32,128,1]{2,0,1:T(8,128)} %copy.49) | copy-start | bytes 49156
  211.1 11.3 %copy-start.32 = (f32[32,128,1]{2,0,1:T(8,128)S(1)}, f32[32,128,1]{2,0,1:T(8,128)}, u32[]{:S(2)}) copy-start(f32[32,128,1]{2,0,1:T(8,128)} %copy.50) | copy-start | bytes 49156
  212.1 6.3 %collective-permute-start.22 = (f32[32,1,130]{2,0,1:T(8,128)S(1)}, f32[32,1,130]{2,0,1:T(8,128)S(1)}, u32[]{:S(2)}, u32[]{:S(2)}) collective-permute-start(f32[32,1,130]{2,0,1:T(8,128)S(1)} %get-tuple-element.12), channel_id=1, source_target_pairs={{0,16},{16,32},{32,48},{48,64},{64,80},{80,96},{96,112},{1,17},{17... | collective-permute-start | bytes 49928 | tf_op jit(solution)/shard_map/ppermute | solution.py:19
  214.5 7.9 %collective-permute-start.23 = (f32[32,1,130]{2,0,1:T(8,128)S(1)}, f32[32,1,130]{2,0,1:T(8,128)S(1)}, u32[]{:S(2)}, u32[]{:S(2)}) collective-permute-start(f32[32,1,130]{2,0,1:T(8,128)S(1)} %get-tuple-element.13), channel_id=1, source_target_pairs={{16,0},{32,16},{48,32},{64,48},{80,64},{96,80},{112,96},{17,1},{33... | collective-permute-start | bytes 49928 | tf_op jit(solution)/shard_map/ppermute | solution.py:21
  232.6 10.8 %collective-permute-start.24 = (f32[32,128,1]{1,0,2:T(8,128)S(1)}, f32[32,128,1]{1,0,2:T(8,128)S(1)}, u32[]{:S(2)}, u32[]{:S(2)}) collective-permute-start(f32[32,128,1]{1,0,2:T(8,128)S(1)} %copy.51), channel_id=1, source_target_pairs={{0,1},{1,2},{2,3},{3,4},{4,5},{5,6},{6,7},{7,8},{8,9},{9,10},{10,1... | collective-permute-start | bytes 49160 | tf_op jit(solution)/shard_map/ppermute | solution.py:19
  235.3 11.1 %collective-permute-start.25 = (f32[32,128,1]{1,0,2:T(8,128)S(1)}, f32[32,128,1]{1,0,2:T(8,128)S(1)}, u32[]{:S(2)}, u32[]{:S(2)}) collective-permute-start(f32[32,128,1]{1,0,2:T(8,128)S(1)} %copy.52), channel_id=1, source_target_pairs={{1,0},{2,1},{3,2},{4,3},{5,4},{6,5},{7,6},{8,7},{9,8},{10,9},{11,1... | collective-permute-start | bytes 49160 | tf_op jit(solution)/shard_map/ppermute | solution.py:21
  249.3 7.6 %copy-start.3 = (f32[32,128,128]{2,0,1:T(8,128)S(1)}, f32[32,128,128]{2,0,1:T(8,128)}, u32[]{:S(2)}) copy-start(f32[32,128,128]{2,0,1:T(8,128)} %copy-done.1) | copy-start | bytes 6291460
  249.3 11.2 %copy-start.19 = (f32[32,128,1]{2,0,1:T(8,128)S(1)}, f32[32,128,1]{2,0,1:T(8,128)}, u32[]{:S(2)}) copy-start(f32[32,128,1]{2,0,1:T(8,128)} %copy.53) | copy-start | bytes 49156
  249.3 11.2 %copy-start.27 = (f32[32,128,1]{2,0,1:T(8,128)S(1)}, f32[32,128,1]{2,0,1:T(8,128)}, u32[]{:S(2)}) copy-start(f32[32,128,1]{2,0,1:T(8,128)} %copy.54) | copy-start | bytes 49156
  250.3 10.1 %copy-start.13 = (f32[32,128,128]{2,0,1:T(8,128)S(1)}, f32[32,128,128]{2,0,1:T(8,128)}, u32[]{:S(2)}) copy-start(f32[32,128,128]{2,0,1:T(8,128)} %copy-done.12) | copy-start | bytes 6291460
  250.3 7.6 %collective-permute-start.26 = (f32[32,1,130]{2,0,1:T(8,128)S(1)}, f32[32,1,130]{2,0,1:T(8,128)S(1)}, u32[]{:S(2)}, u32[]{:S(2)}) collective-permute-start(f32[32,1,130]{2,0,1:T(8,128)S(1)} %get-tuple-element.10), channel_id=1, source_target_pairs={{0,16},{16,32},{32,48},{48,64},{64,80},{80,96},{96,112},{1,17},{17... | collective-permute-start | bytes 49928 | tf_op jit(solution)/shard_map/ppermute | solution.py:19
  252.5 7.9 %collective-permute-start.27 = (f32[32,1,130]{2,0,1:T(8,128)S(1)}, f32[32,1,130]{2,0,1:T(8,128)S(1)}, u32[]{:S(2)}, u32[]{:S(2)}) collective-permute-start(f32[32,1,130]{2,0,1:T(8,128)S(1)} %get-tuple-element.11), channel_id=1, source_target_pairs={{16,0},{32,16},{48,32},{64,48},{80,64},{96,80},{112,96},{17,1},{33... | collective-permute-start | bytes 49928 | tf_op jit(solution)/shard_map/ppermute | solution.py:21
  270.6 9.1 %collective-permute-start.28 = (f32[32,128,1]{1,0,2:T(8,128)S(1)}, f32[32,128,1]{1,0,2:T(8,128)S(1)}, u32[]{:S(2)}, u32[]{:S(2)}) collective-permute-start(f32[32,128,1]{1,0,2:T(8,128)S(1)} %copy.55), channel_id=1, source_target_pairs={{0,1},{1,2},{2,3},{3,4},{4,5},{5,6},{6,7},{7,8},{8,9},{9,10},{10,1... | collective-permute-start | bytes 49160 | tf_op jit(solution)/shard_map/ppermute | solution.py:19
  273.3 9.3 %collective-permute-start.29 = (f32[32,128,1]{1,0,2:T(8,128)S(1)}, f32[32,128,1]{1,0,2:T(8,128)S(1)}, u32[]{:S(2)}, u32[]{:S(2)}) collective-permute-start(f32[32,128,1]{1,0,2:T(8,128)S(1)} %copy.56), channel_id=1, source_target_pairs={{1,0},{2,1},{3,2},{4,3},{5,4},{6,5},{7,6},{8,7},{9,8},{10,9},{11,1... | collective-permute-start | bytes 49160 | tf_op jit(solution)/shard_map/ppermute | solution.py:21
  285.5 7.3 %copy-start.6 = (f32[32,128,128]{2,0,1:T(8,128)S(1)}, f32[32,128,128]{2,0,1:T(8,128)}, u32[]{:S(2)}) copy-start(f32[32,128,128]{2,0,1:T(8,128)} %copy-done.4) | copy-start | bytes 6291460
  285.5 11.1 %copy-start.28 = (f32[32,128,1]{2,0,1:T(8,128)S(1)}, f32[32,128,1]{2,0,1:T(8,128)}, u32[]{:S(2)}) copy-start(f32[32,128,1]{2,0,1:T(8,128)} %copy.58) | copy-start | bytes 49156
  286.5 10.1 %copy-start.20 = (f32[32,128,1]{2,0,1:T(8,128)S(1)}, f32[32,128,1]{2,0,1:T(8,128)}, u32[]{:S(2)}) copy-start(f32[32,128,1]{2,0,1:T(8,128)} %copy.57) | copy-start | bytes 49156
  286.5 7.3 %collective-permute-start.30 = (f32[32,1,130]{2,0,1:T(8,128)S(1)}, f32[32,1,130]{2,0,1:T(8,128)S(1)}, u32[]{:S(2)}, u32[]{:S(2)}) collective-permute-start(f32[32,1,130]{2,0,1:T(8,128)S(1)} %get-tuple-element.8), channel_id=1, source_target_pairs={{0,16},{16,32},{32,48},{48,64},{64,80},{80,96},{96,112},{1,17},{17... | collective-permute-start | bytes 49928 | tf_op jit(solution)/shard_map/ppermute | solution.py:19
  288.7 7.9 %collective-permute-start.31 = (f32[32,1,130]{2,0,1:T(8,128)S(1)}, f32[32,1,130]{2,0,1:T(8,128)S(1)}, u32[]{:S(2)}, u32[]{:S(2)}) collective-permute-start(f32[32,1,130]{2,0,1:T(8,128)S(1)} %get-tuple-element.9), channel_id=1, source_target_pairs={{16,0},{32,16},{48,32},{64,48},{80,64},{96,80},{112,96},{17,1},{33... | collective-permute-start | bytes 49928 | tf_op jit(solution)/shard_map/ppermute | solution.py:21
  306.8 73.8 %collective-permute-start.32 = (f32[32,128,1]{1,0,2:T(8,128)S(1)}, f32[32,128,1]{1,0,2:T(8,128)}, u32[]{:S(2)}, u32[]{:S(2)}) collective-permute-start(f32[32,128,1]{1,0,2:T(8,128)S(1)} %copy.59), channel_id=1, source_target_pairs={{0,1},{1,2},{2,3},{3,4},{4,5},{5,6},{6,7},{7,8},{8,9},{9,10},{10,1... | collective-permute-start | bytes 49160 | tf_op jit(solution)/shard_map/ppermute | solution.py:19
  310.1 74.1 %collective-permute-start.33 = (f32[32,128,1]{1,0,2:T(8,128)}, f32[32,128,1]{1,0,2:T(8,128)}, u32[]{:S(2)}, u32[]{:S(2)}) collective-permute-start(f32[32,128,1]{1,0,2:T(8,128)} %copy.60), channel_id=1, source_target_pairs={{1,0},{2,1},{3,2},{4,3},{5,4},{6,5},{7,6},{8,7},{9,8},{10,9},{11,1... | collective-permute-start | bytes 49160 | tf_op jit(solution)/shard_map/ppermute | solution.py:21
  387.8 13.4 %copy-start.16 = (f32[32,128,128]{2,0,1:T(8,128)S(1)}, f32[32,128,128]{2,0,1:T(8,128)}, u32[]{:S(2)}) copy-start(f32[32,128,128]{2,0,1:T(8,128)} %copy-done.15) | copy-start | bytes 6291460
  387.8 13.4 %copy-start.18 = (f32[32,128,1]{2,0,1:T(8,128)S(1)}, f32[32,128,1]{2,0,1:T(8,128)}, u32[]{:S(2)}) copy-start(f32[32,128,1]{2,0,1:T(8,128)} %copy.61) | copy-start | bytes 49156
  387.8 13.4 %copy-start.26 = (f32[32,128,1]{2,0,1:T(8,128)S(1)}, f32[32,128,1]{2,0,1:T(8,128)}, u32[]{:S(2)}) copy-start(f32[32,128,1]{2,0,1:T(8,128)} %copy.62) | copy-start | bytes 49156
  388.9 7.2 %collective-permute-start.34 = (f32[32,1,130]{2,0,1:T(8,128)S(1)}, f32[32,1,130]{2,0,1:T(8,128)S(1)}, u32[]{:S(2)}, u32[]{:S(2)}) collective-permute-start(f32[32,1,130]{2,0,1:T(8,128)S(1)} %get-tuple-element.6), channel_id=1, source_target_pairs={{0,16},{16,32},{32,48},{48,64},{64,80},{80,96},{96,112},{1,17},{17... | collective-permute-start | bytes 49928 | tf_op jit(solution)/shard_map/ppermute | solution.py:19
  393.3 7.9 %collective-permute-start.35 = (f32[32,1,130]{2,0,1:T(8,128)S(1)}, f32[32,1,130]{2,0,1:T(8,128)S(1)}, u32[]{:S(2)}, u32[]{:S(2)}) collective-permute-start(f32[32,1,130]{2,0,1:T(8,128)S(1)} %get-tuple-element.7), channel_id=1, source_target_pairs={{16,0},{32,16},{48,32},{64,48},{80,64},{96,80},{112,96},{17,1},{33... | collective-permute-start | bytes 49928 | tf_op jit(solution)/shard_map/ppermute | solution.py:21
  (11 other events, 43.5 us)
where the time goes:
time: 415 us; the launch traced here: 408 us
  local copies, waits for them, and re-layouts  116 us (28%)
  starting transfers between devices  106 us (26%)
  other arithmetic  63.1 us (15%)
  blocking collectives  62.9 us (15%)
  matrix products  30.9 us (7%)
  waiting for transfers between devices  28 us (7%)
    ppermute x18, starting transfers between devices, padded_2(): lax.ppermute(head, axis, [((i + 1) % count, i) for i in range(ends)])  81.6 us
    psum x1, blocking collectives, local(): summed = lax.psum(weight_terms, ('lat', 'lon'))  62.9 us
    slice x17, local copies, waits for them, and re-layouts, padded_2(): lax.slice_in_dim(cells, cells.shape[dim] - width, cells.shape[dim], axis=...  44.4 us
    ppermute x18, waiting for transfers between devices, padded_2(): lax.ppermute(head, axis, [((i + 1) % count, i) for i in range(ends)])  28 us
    mul x9, other arithmetic, laplace(): return -scale_zero * neigh_sum(scale_one * padded, 1, 0)  24.9 us
    ppermute x18, starting transfers between devices, padded_2(): lax.ppermute(tail, axis, [(i, (i + 1) % count) for i in range(ends)])  24.2 us
    ppermute x8, local copies, waits for them, and re-layouts, padded_2(): lax.ppermute(tail, axis, [(i, (i + 1) % count) for i in range(ends)])  24 us
    ppermute x8, local copies, waits for them, and re-layouts, padded_2(): lax.ppermute(head, axis, [((i + 1) % count, i) for i in range(ends)])  23.6 us
  transfers between devices with their start and end apart: 36, of which 8 were waited for; matrix products, arithmetic and copies ran while one was open for 17% of the time, Pallas kernels for 0%

commit v1 on v0

--- a/solution.py
+++ b/solution.py
@@ -89,7 +89,7 @@
             for kept in carried
         ]
     )
-    summed = lax.psum(weight_terms, ("lat", "lon"))
+    summed = jnp.sum(lax.all_gather(weight_terms, ("lat", "lon")), axis=0)
     grid_cells = features.shape[1] * lax.axis_size("lat") * features.shape[2] * lax.axis_size("lon")
     weight_grad = summed * (1.0 / math.sqrt(grid_cells))
 

time: 415 us -> 431 us (1.039)
  the two profiles are of different devices: /device:TPU:96 before, /device:TPU:1 now
where the time goes in v1:
time: 431 us; the launch traced here: 424 us
  local copies, waits for them, and re-layouts  113 us (26%)
  starting transfers between devices  104 us (24%)
  waiting for transfers between devices  97 us (23%)
  other arithmetic  68 us (16%)
  matrix products  26.5 us (6%)
  between operations  15 us (3%)
    all_gather x1, waiting for transfers between devices, local(): summed = jnp.sum(lax.all_gather(weight_terms, ('lat', 'lon')), axis=0)  71.4 us
    ppermute x18, starting transfers between devices, padded_2(): lax.ppermute(head, axis, [((i + 1) % count, i) for i in range(ends)])  61.9 us
    slice x17, local copies, waits for them, and re-layouts, padded_2(): lax.slice_in_dim(cells, cells.shape[dim] - width, cells.shape[dim], axis=...  43.6 us
    ppermute x18, starting transfers between devices, padded_2(): lax.ppermute(tail, axis, [(i, (i + 1) % count) for i in range(ends)])  42 us
    ppermute x18, waiting for transfers between devices, padded_2(): lax.ppermute(head, axis, [((i + 1) % count, i) for i in range(ends)])  25.5 us
    mul x9, other arithmetic, laplace(): return -scale_zero * neigh_sum(scale_one * padded, 1, 0)  24.8 us
    ppermute x8, local copies, waits for them, and re-layouts, padded_2(): lax.ppermute(tail, axis, [(i, (i + 1) % count) for i in range(ends)])  23.1 us
    ppermute x8, local copies, waits for them, and re-layouts, padded_2(): lax.ppermute(head, axis, [((i + 1) % count, i) for i in range(ends)])  22.9 us
  transfers between devices with their start and end apart: 37, of which 10 were waited for; matrix products, arithmetic and copies ran while one was open for 27% of the time, Pallas kernels for 0%

profile of v1, /device:TPU:1, one launch (start us, length us, event | category | flops | bytes accessed | tf_op | source)
XLA Modules:
  0.0 423.9 jit_solution(9618326960962907177)
XLA Ops:
  8.2 2.8 collective-permute-start
  15.1 3.5 collective-permute-start.2
  19.9 2.8 fusion.75
  31.8 2.9 copy.24
  34.6 2.8 copy.25
  38.5 4.4 %collective-permute-start.6 = (f32[32,1,130]{2,0,1:T(8,128)S(1)}, f32[32,1,130]{2,0,1:T(8,128)S(1)}, u32[]{:S(2)}, u32[]{:S(2)}) collective-permute-start(f32[32,1,130]{2,0,1:T(8,128)S(1)} %get-tuple-element.20), channel_id=1, source_target_pairs={{0,16},{16,32},{32,48},{48,64},{64,80},{80,96},{96,112},{1,17},{17... | collective-permute-start | bytes 49928 | tf_op jit(solution)/shard_map/ppermute | solution.py:19
  44.6 3.2 collective-permute-done.7
  52.5 2.8 fusion.74
  61.2 6.1 %collective-permute-start.9 = (f32[32,128,1]{1,0,2:T(8,128)S(1)}, f32[32,128,1]{1,0,2:T(8,128)S(1)}, u32[]{:S(2)}, u32[]{:S(2)}) collective-permute-start(f32[32,128,1]{1,0,2:T(8,128)S(1)} %copy.28), channel_id=1, source_target_pairs={{1,0},{2,1},{3,2},{4,3},{5,4},{6,5},{7,6},{8,7},{9,8},{10,9},{11,1... | collective-permute-start | bytes 49160 | tf_op jit(solution)/shard_map/ppermute | solution.py:21
  67.3 2.9 copy.29
  70.2 2.9 copy.30
  74.1 3.7 collective-permute-start.10
  79.5 3.3 collective-permute-done.11
  85.2 4.1 fusion.25
  89.3 2.8 fusion.73
  92.1 2.7 copy.32
  94.9 2.7 copy.33
  97.6 6.7 %collective-permute-start.13 = (f32[32,128,1]{1,0,2:T(8,128)S(1)}, f32[32,128,1]{1,0,2:T(8,128)S(1)}, u32[]{:S(2)}, u32[]{:S(2)}) collective-permute-start(f32[32,128,1]{1,0,2:T(8,128)S(1)} %copy.33), channel_id=1, source_target_pairs={{1,0},{2,1},{3,2},{4,3},{5,4},{6,5},{7,6},{8,7},{9,8},{10,9},{11,1... | collective-permute-start | bytes 49160 | tf_op jit(solution)/shard_map/ppermute | solution.py:21
  106.4 2.9 copy.34
  109.3 2.9 copy.35
  113.2 5.6 %collective-permute-start.14 = (f32[32,1,130]{2,0,1:T(8,128)S(1)}, f32[32,1,130]{2,0,1:T(8,128)S(1)}, u32[]{:S(2)}, u32[]{:S(2)}) collective-permute-start(f32[32,1,130]{2,0,1:T(8,128)S(1)} %get-tuple-element.16), channel_id=1, source_target_pairs={{0,16},{16,32},{32,48},{48,64},{64,80},{80,96},{96,112},{1,17},{17... | collective-permute-start | bytes 49928 | tf_op jit(solution)/shard_map/ppermute | solution.py:19
  124.0 3.8 maximum_multiply_fusion.2
  127.9 11.7 %fusion.22 = f32[32,128,128]{2,0,1:T(8,128)S(1)} fusion(f32[32,130,130]{2,0,1:T(8,128)} %maximum_multiply_fusion.2, f32[128,128]{1,0:T(8,128)S(1)} %slice_negate_fusion, f32[32,130,130]{2,0,1:T(8,128)S(1)} %bitcast.103), kind=kLoop, calls=%fused_computation.56 | loop fusion | flops 7340032 | bytes 27328512 | tf_op jit(solution)/shard_map/sub | solution.py:76
  139.6 2.8 fusion.72
  142.4 2.7 copy.37
  145.1 2.7 copy.38
  147.7 6.5 %collective-permute-start.17 = (f32[32,128,1]{1,0,2:T(8,128)S(1)}, f32[32,128,1]{1,0,2:T(8,128)S(1)}, u32[]{:S(2)}, u32[]{:S(2)}) collective-permute-start(f32[32,128,1]{1,0,2:T(8,128)S(1)} %copy.38), channel_id=1, source_target_pairs={{1,0},{2,1},{3,2},{4,3},{5,4},{6,5},{7,6},{8,7},{9,8},{10,9},{11,1... | collective-permute-start | bytes 49160 | tf_op jit(solution)/shard_map/ppermute | solution.py:21
  156.2 2.9 copy.39
  159.1 2.8 copy.40
  162.9 3.7 collective-permute-start.18
  171.9 3.8 maximum_multiply_fusion.3
  175.7 10.2 %fusion.19 = bf16[32,128,128]{2,0,1:T(8,128)(2,1)S(1)} fusion(f32[32,128,128]{2,0,1:T(8,128)S(1)} %fusion.25, f32[32,130,130]{2,0,1:T(8,128)} %maximum_multiply_fusion.3, f32[128,128]{1,0:T(8,128)S(1)} %slice_negate_fusion), kind=kLoop, calls=%fused_computation.48 | loop fusion | flops 4718592 | bytes 15794176 | tf_op jit(solution)/shard_map/convert_element_type | solution.py:68
  185.9 5.3 %fusion.27 = bf16[32,128,128]{2,0,1:T(8,128)(2,1)S(1)} fusion(f32[128,128,32]{1,2,0:T(8,128)} %fusion.34, f32[128,128,32]{1,2,0:T(8,128)} %fusion.37, f32[128,128,32]{1,2,0:T(8,128)} %fusion.43, f32[128,128,32]{1,2,0:T(8,128)} %fusion.40, bf16[32,128,128]{2,0,1:T(8,128)(2,1)S(1)} %fusion.19, bf16[32,128,128]{2,1,0:T(8,128)(2,1)} %param.5, ...), kind=kOutput, calls=%fused_computation.76 | convolution fusion | flops 38273024 | bytes 11542528 | tf_op jit(solution)/shard_map/cd,cij->dij/dot_general | solution.py:81
  197.8 2.7 fusion.71
  203.3 2.7 copy.48
  205.9 6.7 %collective-permute-start.21 = (f32[32,128,1]{1,0,2:T(8,128)S(1)}, f32[32,128,1]{1,0,2:T(8,128)S(1)}, u32[]{:S(2)}, u32[]{:S(2)}) collective-permute-start(f32[32,128,1]{1,0,2:T(8,128)S(1)} %copy.48), channel_id=1, source_target_pairs={{1,0},{2,1},{3,2},{4,3},{5,4},{6,5},{7,6},{8,7},{9,8},{10,9},{11,1... | collective-permute-start | bytes 49160 | tf_op jit(solution)/shard_map/ppermute | solution.py:21
  212.6 2.9 copy.49
  215.5 2.9 copy.50
  219.5 3.9 collective-permute-start.22
  224.7 3.6 collective-permute-done.23
  233.1 2.7 fusion.70
  235.8 2.7 copy.51
  238.5 2.7 copy.52
  241.1 6.5 %collective-permute-start.25 = (f32[32,128,1]{1,0,2:T(8,128)S(1)}, f32[32,128,1]{1,0,2:T(8,128)S(1)}, u32[]{:S(2)}, u32[]{:S(2)}) collective-permute-start(f32[32,128,1]{1,0,2:T(8,128)S(1)} %copy.52), channel_id=1, source_target_pairs={{1,0},{2,1},{3,2},{4,3},{5,4},{6,5},{7,6},{8,7},{9,8},{10,9},{11,1... | collective-permute-start | bytes 49160 | tf_op jit(solution)/shard_map/ppermute | solution.py:21
  247.7 2.9 copy.53
  250.5 2.9 copy.54
  254.5 4.4 %collective-permute-start.26 = (f32[32,1,130]{2,0,1:T(8,128)S(1)}, f32[32,1,130]{2,0,1:T(8,128)S(1)}, u32[]{:S(2)}, u32[]{:S(2)}) collective-permute-start(f32[32,1,130]{2,0,1:T(8,128)S(1)} %get-tuple-element.10), channel_id=1, source_target_pairs={{0,16},{16,32},{32,48},{48,64},{64,80},{80,96},{96,112},{1,17},{17... | collective-permute-start | bytes 49928 | tf_op jit(solution)/shard_map/ppermute | solution.py:19
  260.5 4.3 %collective-permute-done.27 = f32[32,1,130]{2,0,1:T(8,128)S(1)} collective-permute-done((f32[32,1,130]{2,0,1:T(8,128)S(1)}, f32[32,1,130]{2,0,1:T(8,128)S(1)}, u32[]{:S(2)}, u32[]{:S(2)}) %collective-permute-start.27) | collective-permute-done | bytes 16672 | tf_op jit(solution)/shard_map/ppermute | solution.py:21
  271.7 2.7 copy.55
  275.7 6.1 %collective-permute-start.29 = (f32[32,128,1]{1,0,2:T(8,128)S(1)}, f32[32,128,1]{1,0,2:T(8,128)S(1)}, u32[]{:S(2)}, u32[]{:S(2)}) collective-permute-start(f32[32,128,1]{1,0,2:T(8,128)S(1)} %copy.56), channel_id=1, source_target_pairs={{1,0},{2,1},{3,2},{4,3},{5,4},{6,5},{7,6},{8,7},{9,8},{10,9},{11,1... | collective-permute-start | bytes 49160 | tf_op jit(solution)/shard_map/ppermute | solution.py:21
  281.8 2.9 copy.57
  284.6 2.9 copy.58
  288.5 4.6 %collective-permute-start.30 = (f32[32,1,130]{2,0,1:T(8,128)S(1)}, f32[32,1,130]{2,0,1:T(8,128)S(1)}, u32[]{:S(2)}, u32[]{:S(2)}) collective-permute-start(f32[32,1,130]{2,0,1:T(8,128)S(1)} %get-tuple-element.8), channel_id=1, source_target_pairs={{0,16},{16,32},{32,48},{48,64},{64,80},{80,96},{96,112},{1,17},{17... | collective-permute-start | bytes 49928 | tf_op jit(solution)/shard_map/ppermute | solution.py:19
  294.7 3.6 collective-permute-done.31
  303.1 2.7 fusion.68
  305.8 2.7 copy.59
  308.6 2.7 copy.60
  311.2 6.6 %collective-permute-start.33 = (f32[32,128,1]{1,0,2:T(8,128)S(1)}, f32[32,128,1]{1,0,2:T(8,128)S(1)}, u32[]{:S(2)}, u32[]{:S(2)}) collective-permute-start(f32[32,128,1]{1,0,2:T(8,128)S(1)} %copy.60), channel_id=1, source_target_pairs={{1,0},{2,1},{3,2},{4,3},{5,4},{6,5},{7,6},{8,7},{9,8},{10,9},{11,1... | collective-permute-start | bytes 49160 | tf_op jit(solution)/shard_map/ppermute | solution.py:21
  317.8 2.9 copy.61
  320.7 2.9 copy.62
  324.6 3.8 collective-permute-start.34
  330.0 3.3 collective-permute-done.35
  339.5 71.4 %all-gather.3.cloned.1.call-done = f32[640,32,32]{2,1,0:T(8,128)} async-done(((f32[5,32,32]{2,1,0:T(8,128)}), f32[640,32,32]{2,1,0:T(8,128)}) %all-gather.3.cloned.1.call-update) | async-done | bytes 2621456 | tf_op jit(solution)/shard_map/all_gather | solution.py:92
  411.0 5.2 %reduce_sum.9 = f32[5,32,32]{2,1,0:T(8,128)S(1)} reduce(f32[128,5,32,32]{3,2,1,0:T(8,128)} %bitcast.104, f32[]{:T(128)} %constant.1.clone.1), dimensions={0}, to_apply=%region_0.0 | reduce | flops 650240 | bytes 2641924 | tf_op jit(solution)/shard_map/reduce_sum | solution.py:92
  (176 shorter events, 94.8 us)
Async XLA Ops:
  7.2 7.8 %copy-start.34 = (s32[128,128]{1,0:T(8,128)S(1)}, s32[128,128]{1,0:T(8,128)}, u32[]{:S(2)}) copy-start(s32[128,128]{1,0:T(8,128)} %param.6) | copy-start | bytes 196612
  7.2 403.8 %all-gather.3.cloned.1.call-start = ((), (), s32[]{:S(2)}) async-start(), calls=%async_computation | async-start | bytes 10567680 | tf_op jit(solution)/shard_map/all_gather | solution.py:92
  8.2 5.6 %collective-permute-start = (s32[128,3]{1,0:T(8,128)S(1)}, s32[128,3]{1,0:T(8,128)S(1)}, u32[]{:S(2)}, u32[]{:S(2)}) collective-permute-start(s32[128,3]{1,0:T(8,128)S(1)} %get-tuple-element.40), channel_id=1, source_target_pairs={{0,1},{1,2},{2,3},{3,4},{4,5},{5,6},{6,7},{7,8},{8,9},{9,10},{10,1... | collective-permute-start | bytes 4616 | tf_op jit(solution)/shard_map/ppermute | solution.py:19
  11.0 4.0 collective-permute-start.1
  15.1 16.3 %collective-permute-start.2 = (s32[3,134]{1,0:T(4,128)S(1)}, s32[3,134]{1,0:T(4,128)S(1)}, u32[]{:S(2)}, u32[]{:S(2)}) collective-permute-start(s32[3,134]{1,0:T(4,128)S(1)} %get-tuple-element.38), channel_id=1, source_target_pairs={{0,16},{16,32},{32,48},{48,64},{64,80},{80,96},{96,112},{1,17},{17... | collective-permute-start | bytes 4832 | tf_op jit(solution)/shard_map/ppermute | solution.py:19
  18.6 12.8 %collective-permute-start.3 = (s32[3,134]{1,0:T(4,128)S(1)}, s32[3,134]{1,0:T(4,128)S(1)}, u32[]{:S(2)}, u32[]{:S(2)}) collective-permute-start(s32[3,134]{1,0:T(4,128)S(1)} %get-tuple-element.39), channel_id=1, source_target_pairs={{16,0},{32,16},{48,32},{64,48},{80,64},{96,80},{112,96},{17,1},{33... | collective-permute-start | bytes 4832 | tf_op jit(solution)/shard_map/ppermute | solution.py:21
  25.3 6.5 %collective-permute-start.4 = (f32[32,128,1]{1,0,2:T(8,128)S(1)}, f32[32,128,1]{1,0,2:T(8,128)S(1)}, u32[]{:S(2)}, u32[]{:S(2)}) collective-permute-start(f32[32,128,1]{1,0,2:T(8,128)S(1)} %copy.22), channel_id=1, source_target_pairs={{0,1},{1,2},{2,3},{3,4},{4,5},{5,6},{6,7},{7,8},{8,9},{9,10},{10,1... | collective-permute-start | bytes 49160 | tf_op jit(solution)/shard_map/ppermute | solution.py:19
  28.9 5.8 %collective-permute-start.5 = (f32[32,128,1]{1,0,2:T(8,128)S(1)}, f32[32,128,1]{1,0,2:T(8,128)S(1)}, u32[]{:S(2)}, u32[]{:S(2)}) collective-permute-start(f32[32,128,1]{1,0,2:T(8,128)S(1)} %copy.23), channel_id=1, source_target_pairs={{1,0},{2,1},{3,2},{4,3},{5,4},{6,5},{7,6},{8,7},{9,8},{10,9},{11,1... | collective-permute-start | bytes 49160 | tf_op jit(solution)/shard_map/ppermute | solution.py:21
  37.5 10.3 %copy-start.15 = (f32[32,128,1]{2,0,1:T(8,128)S(1)}, f32[32,128,1]{2,0,1:T(8,128)}, u32[]{:S(2)}) copy-start(f32[32,128,1]{2,0,1:T(8,128)} %copy.24) | copy-start | bytes 49156
  37.5 10.3 %copy-start.23 = (f32[32,128,1]{2,0,1:T(8,128)S(1)}, f32[32,128,1]{2,0,1:T(8,128)}, u32[]{:S(2)}) copy-start(f32[32,128,1]{2,0,1:T(8,128)} %copy.25) | copy-start | bytes 49156
  38.5 6.1 %collective-permute-start.6 = (f32[32,1,130]{2,0,1:T(8,128)S(1)}, f32[32,1,130]{2,0,1:T(8,128)S(1)}, u32[]{:S(2)}, u32[]{:S(2)}) collective-permute-start(f32[32,1,130]{2,0,1:T(8,128)S(1)} %get-tuple-element.20), channel_id=1, source_target_pairs={{0,16},{16,32},{32,48},{48,64},{64,80},{80,96},{96,112},{1,17},{17... | collective-permute-start | bytes 49928 | tf_op jit(solution)/shard_map/ppermute | solution.py:19
  42.9 4.9 %collective-permute-start.7 = (f32[32,1,130]{2,0,1:T(8,128)S(1)}, f32[32,1,130]{2,0,1:T(8,128)S(1)}, u32[]{:S(2)}, u32[]{:S(2)}) collective-permute-start(f32[32,1,130]{2,0,1:T(8,128)S(1)} %get-tuple-element.21), channel_id=1, source_target_pairs={{16,0},{32,16},{48,32},{64,48},{80,64},{96,80},{112,96},{17,1},{33... | collective-permute-start | bytes 49928 | tf_op jit(solution)/shard_map/ppermute | solution.py:21
  52.5 30.2 %copy-start.1 = (f32[32,128,128]{2,0,1:T(8,128)}, f32[32,128,128]{2,0,1:T(8,128)S(1)}, u32[]{:S(2)}) copy-start(f32[32,128,128]{2,0,1:T(8,128)S(1)} %fusion.26) | copy-start | bytes 6291460
  57.9 9.3 %collective-permute-start.8 = (f32[32,128,1]{1,0,2:T(8,128)S(1)}, f32[32,128,1]{1,0,2:T(8,128)S(1)}, u32[]{:S(2)}, u32[]{:S(2)}) collective-permute-start(f32[32,128,1]{1,0,2:T(8,128)S(1)} %copy.27), channel_id=1, source_target_pairs={{0,1},{1,2},{2,3},{3,4},{4,5},{5,6},{6,7},{7,8},{8,9},{9,10},{10,1... | collective-permute-start | bytes 49160 | tf_op jit(solution)/shard_map/ppermute | solution.py:19
  61.2 9.0 %collective-permute-start.9 = (f32[32,128,1]{1,0,2:T(8,128)S(1)}, f32[32,128,1]{1,0,2:T(8,128)S(1)}, u32[]{:S(2)}, u32[]{:S(2)}) collective-permute-start(f32[32,128,1]{1,0,2:T(8,128)S(1)} %copy.28), channel_id=1, source_target_pairs={{1,0},{2,1},{3,2},{4,3},{5,4},{6,5},{7,6},{8,7},{9,8},{10,9},{11,1... | collective-permute-start | bytes 49160 | tf_op jit(solution)/shard_map/ppermute | solution.py:21
  73.1 9.6 %copy-start.19 = (f32[32,128,1]{2,0,1:T(8,128)S(1)}, f32[32,128,1]{2,0,1:T(8,128)}, u32[]{:S(2)}) copy-start(f32[32,128,1]{2,0,1:T(8,128)} %copy.29) | copy-start | bytes 49156
  73.1 9.6 %copy-start.27 = (f32[32,128,1]{2,0,1:T(8,128)S(1)}, f32[32,128,1]{2,0,1:T(8,128)}, u32[]{:S(2)}) copy-start(f32[32,128,1]{2,0,1:T(8,128)} %copy.30) | copy-start | bytes 49156
  74.1 5.3 %collective-permute-start.10 = (f32[32,1,130]{2,0,1:T(8,128)S(1)}, f32[32,1,130]{2,0,1:T(8,128)S(1)}, u32[]{:S(2)}, u32[]{:S(2)}) collective-permute-start(f32[32,1,130]{2,0,1:T(8,128)S(1)} %get-tuple-element.18), channel_id=1, source_target_pairs={{0,16},{16,32},{32,48},{48,64},{64,80},{80,96},{96,112},{1,17},{17... | collective-permute-start | bytes 49928 | tf_op jit(solution)/shard_map/ppermute | solution.py:19
  77.8 7.4 %copy-start.31 = (bf16[32,128,128]{2,1,0:T(8,128)(2,1)S(1)}, bf16[32,128,128]{2,1,0:T(8,128)(2,1)}, u32[]{:S(2)}) copy-start(bf16[32,128,128]{2,1,0:T(8,128)(2,1)} %param.4) | copy-start | bytes 3145732
  77.8 4.9 %collective-permute-start.11 = (f32[32,1,130]{2,0,1:T(8,128)S(1)}, f32[32,1,130]{2,0,1:T(8,128)S(1)}, u32[]{:S(2)}, u32[]{:S(2)}) collective-permute-start(f32[32,1,130]{2,0,1:T(8,128)S(1)} %get-tuple-element.19), channel_id=1, source_target_pairs={{16,0},{32,16},{48,32},{64,48},{80,64},{96,80},{112,96},{17,1},{33... | collective-permute-start | bytes 49928 | tf_op jit(solution)/shard_map/ppermute | solution.py:21
  92.1 12.2 %copy-start.32 = (bf16[32,128,128]{2,1,0:T(8,128)(2,1)S(1)}, bf16[32,128,128]{2,1,0:T(8,128)(2,1)}, u32[]{:S(2)}) copy-start(bf16[32,128,128]{2,1,0:T(8,128)(2,1)} %param.4) | copy-start | bytes 3145732
  92.1 12.2 %copy-start.36 = (bf16[5,32,32]{2,1,0:T(8,128)(2,1)S(1)}, bf16[5,32,32]{2,1,0:T(8,128)(2,1)}, u32[]{:S(2)}) copy-start(bf16[5,32,32]{2,1,0:T(8,128)(2,1)} %param.7) | copy-start | bytes 30724
  94.8 11.5 %collective-permute-start.12 = (f32[32,128,1]{1,0,2:T(8,128)S(1)}, f32[32,128,1]{1,0,2:T(8,128)S(1)}, u32[]{:S(2)}, u32[]{:S(2)}) collective-permute-start(f32[32,128,1]{1,0,2:T(8,128)S(1)} %copy.32), channel_id=1, source_target_pairs={{0,1},{1,2},{2,3},{3,4},{4,5},{5,6},{6,7},{7,8},{8,9},{9,10},{10,1... | collective-permute-start | bytes 49160 | tf_op jit(solution)/shard_map/ppermute | solution.py:19
  97.6 11.8 %collective-permute-start.13 = (f32[32,128,1]{1,0,2:T(8,128)S(1)}, f32[32,128,1]{1,0,2:T(8,128)S(1)}, u32[]{:S(2)}, u32[]{:S(2)}) collective-permute-start(f32[32,128,1]{1,0,2:T(8,128)S(1)} %copy.33), channel_id=1, source_target_pairs={{1,0},{2,1},{3,2},{4,3},{5,4},{6,5},{7,6},{8,7},{9,8},{10,9},{11,1... | collective-permute-start | bytes 49160 | tf_op jit(solution)/shard_map/ppermute | solution.py:21
  112.2 8.6 %copy-start.2 = (f32[32,128,128]{2,0,1:T(8,128)S(1)}, f32[32,128,128]{2,0,1:T(8,128)}, u32[]{:S(2)}) copy-start(f32[32,128,128]{2,0,1:T(8,128)} %copy-done.1) | copy-start | bytes 6291460
  113.2 9.4 %collective-permute-start.14 = (f32[32,1,130]{2,0,1:T(8,128)S(1)}, f32[32,1,130]{2,0,1:T(8,128)S(1)}, u32[]{:S(2)}, u32[]{:S(2)}) collective-permute-start(f32[32,1,130]{2,0,1:T(8,128)S(1)} %get-tuple-element.16), channel_id=1, source_target_pairs={{0,16},{16,32},{32,48},{48,64},{64,80},{80,96},{96,112},{1,17},{17... | collective-permute-start | bytes 49928 | tf_op jit(solution)/shard_map/ppermute | solution.py:19
  118.8 5.2 %copy-start.17 = (f32[32,128,1]{2,0,1:T(8,128)S(1)}, f32[32,128,1]{2,0,1:T(8,128)}, u32[]{:S(2)}) copy-start(f32[32,128,1]{2,0,1:T(8,128)} %copy.34) | copy-start | bytes 49156
  118.8 5.2 %collective-permute-start.15 = (f32[32,1,130]{2,0,1:T(8,128)S(1)}, f32[32,1,130]{2,0,1:T(8,128)S(1)}, u32[]{:S(2)}, u32[]{:S(2)}) collective-permute-start(f32[32,1,130]{2,0,1:T(8,128)S(1)} %get-tuple-element.17), channel_id=1, source_target_pairs={{16,0},{32,16},{48,32},{64,48},{80,64},{96,80},{112,96},{17,1},{33... | collective-permute-start | bytes 49928 | tf_op jit(solution)/shard_map/ppermute | solution.py:21
  120.8 7.1 %slice-start = ((s8[4259840]{0:T(1024)(128)(4,1)}), s8[4194304]{0:T(1024)(128)(4,1)S(1)}, s32[]{:S(2)}) async-start(s8[4259840]{0:T(1024)(128)(4,1)} %bitcast.102), calls=%async_computation.1 | async-start | bytes 8388608
  122.6 5.3 %slice-start.1 = ((s8[4259840]{0:T(1024)(128)(4,1)}), s8[65536]{0:T(1024)(128)(4,1)S(1)}, s32[]{:S(2)}) async-start(s8[4259840]{0:T(1024)(128)(4,1)} %bitcast.102), calls=%async_computation.2 | async-start | bytes 131072
  145.0 11.2 %collective-permute-start.16 = (f32[32,128,1]{1,0,2:T(8,128)S(1)}, f32[32,128,1]{1,0,2:T(8,128)S(1)}, u32[]{:S(2)}, u32[]{:S(2)}) collective-permute-start(f32[32,128,1]{1,0,2:T(8,128)S(1)} %copy.37), channel_id=1, source_target_pairs={{0,1},{1,2},{2,3},{3,4},{4,5},{5,6},{6,7},{7,8},{8,9},{9,10},{10,1... | collective-permute-start | bytes 49160 | tf_op jit(solution)/shard_map/ppermute | solution.py:19
  147.7 11.3 %collective-permute-start.17 = (f32[32,128,1]{1,0,2:T(8,128)S(1)}, f32[32,128,1]{1,0,2:T(8,128)S(1)}, u32[]{:S(2)}, u32[]{:S(2)}) collective-permute-start(f32[32,128,1]{1,0,2:T(8,128)S(1)} %copy.38), channel_id=1, source_target_pairs={{1,0},{2,1},{3,2},{4,3},{5,4},{6,5},{7,6},{8,7},{9,8},{10,9},{11,1... | collective-permute-start | bytes 49160 | tf_op jit(solution)/shard_map/ppermute | solution.py:21
  161.9 6.5 %copy-start.5 = (f32[32,128,128]{2,0,1:T(8,128)S(1)}, f32[32,128,128]{2,0,1:T(8,128)}, u32[]{:S(2)}) copy-start(f32[32,128,128]{2,0,1:T(8,128)} %copy-done.4) | copy-start | bytes 6291460
  162.9 7.3 %collective-permute-start.18 = (f32[32,1,130]{2,0,1:T(8,128)S(1)}, f32[32,1,130]{2,0,1:T(8,128)S(1)}, u32[]{:S(2)}, u32[]{:S(2)}) collective-permute-start(f32[32,1,130]{2,0,1:T(8,128)S(1)} %get-tuple-element.14), channel_id=1, source_target_pairs={{0,16},{16,32},{32,48},{48,64},{64,80},{80,96},{96,112},{1,17},{17... | collective-permute-start | bytes 49928 | tf_op jit(solution)/shard_map/ppermute | solution.py:19
  166.7 5.2 %collective-permute-start.19 = (f32[32,1,130]{2,0,1:T(8,128)S(1)}, f32[32,1,130]{2,0,1:T(8,128)S(1)}, u32[]{:S(2)}, u32[]{:S(2)}) collective-permute-start(f32[32,1,130]{2,0,1:T(8,128)S(1)} %get-tuple-element.15), channel_id=1, source_target_pairs={{16,0},{32,16},{48,32},{64,48},{80,64},{96,80},{112,96},{17,1},{33... | collective-permute-start | bytes 49928 | tf_op jit(solution)/shard_map/ppermute | solution.py:21
  185.9 5.3 %copy-start.33 = (bf16[32,128,128]{2,1,0:T(8,128)(2,1)S(1)}, bf16[32,128,128]{2,1,0:T(8,128)(2,1)}, u32[]{:S(2)}) copy-start(bf16[32,128,128]{2,1,0:T(8,128)(2,1)} %param.4) | copy-start | bytes 3145732
  203.2 9.4 %collective-permute-start.20 = (f32[32,128,1]{1,0,2:T(8,128)S(1)}, f32[32,128,1]{1,0,2:T(8,128)S(1)}, u32[]{:S(2)}, u32[]{:S(2)}) collective-permute-start(f32[32,128,1]{1,0,2:T(8,128)S(1)} %copy.47), channel_id=1, source_target_pairs={{0,1},{1,2},{2,3},{3,4},{4,5},{5,6},{6,7},{7,8},{8,9},{9,10},{10,1... | collective-permute-start | bytes 49160 | tf_op jit(solution)/shard_map/ppermute | solution.py:19
  205.9 9.6 %collective-permute-start.21 = (f32[32,128,1]{1,0,2:T(8,128)S(1)}, f32[32,128,1]{1,0,2:T(8,128)S(1)}, u32[]{:S(2)}, u32[]{:S(2)}) collective-permute-start(f32[32,128,1]{1,0,2:T(8,128)S(1)} %copy.48), channel_id=1, source_target_pairs={{1,0},{2,1},{3,2},{4,3},{5,4},{6,5},{7,6},{8,7},{9,8},{10,9},{11,1... | collective-permute-start | bytes 49160 | tf_op jit(solution)/shard_map/ppermute | solution.py:21
  218.5 9.9 %copy-start.20 = (f32[32,128,1]{2,0,1:T(8,128)S(1)}, f32[32,128,1]{2,0,1:T(8,128)}, u32[]{:S(2)}) copy-start(f32[32,128,1]{2,0,1:T(8,128)} %copy.49) | copy-start | bytes 49156
  218.5 9.9 %copy-start.28 = (f32[32,128,1]{2,0,1:T(8,128)S(1)}, f32[32,128,1]{2,0,1:T(8,128)}, u32[]{:S(2)}) copy-start(f32[32,128,1]{2,0,1:T(8,128)} %copy.50) | copy-start | bytes 49156
  219.5 5.2 %collective-permute-start.22 = (f32[32,1,130]{2,0,1:T(8,128)S(1)}, f32[32,1,130]{2,0,1:T(8,128)S(1)}, u32[]{:S(2)}, u32[]{:S(2)}) collective-permute-start(f32[32,1,130]{2,0,1:T(8,128)S(1)} %get-tuple-element.12), channel_id=1, source_target_pairs={{0,16},{16,32},{32,48},{48,64},{64,80},{80,96},{96,112},{1,17},{17... | collective-permute-start | bytes 49928 | tf_op jit(solution)/shard_map/ppermute | solution.py:19
  223.4 4.9 %collective-permute-start.23 = (f32[32,1,130]{2,0,1:T(8,128)S(1)}, f32[32,1,130]{2,0,1:T(8,128)S(1)}, u32[]{:S(2)}, u32[]{:S(2)}) collective-permute-start(f32[32,1,130]{2,0,1:T(8,128)S(1)} %get-tuple-element.13), channel_id=1, source_target_pairs={{16,0},{32,16},{48,32},{64,48},{80,64},{96,80},{112,96},{17,1},{33... | collective-permute-start | bytes 49928 | tf_op jit(solution)/shard_map/ppermute | solution.py:21
  238.4 9.3 %collective-permute-start.24 = (f32[32,128,1]{1,0,2:T(8,128)S(1)}, f32[32,128,1]{1,0,2:T(8,128)S(1)}, u32[]{:S(2)}, u32[]{:S(2)}) collective-permute-start(f32[32,128,1]{1,0,2:T(8,128)S(1)} %copy.51), channel_id=1, source_target_pairs={{0,1},{1,2},{2,3},{3,4},{4,5},{5,6},{6,7},{7,8},{8,9},{9,10},{10,1... | collective-permute-start | bytes 49160 | tf_op jit(solution)/shard_map/ppermute | solution.py:19
  241.1 9.4 %collective-permute-start.25 = (f32[32,128,1]{1,0,2:T(8,128)S(1)}, f32[32,128,1]{1,0,2:T(8,128)S(1)}, u32[]{:S(2)}, u32[]{:S(2)}) collective-permute-start(f32[32,128,1]{1,0,2:T(8,128)S(1)} %copy.52), channel_id=1, source_target_pairs={{1,0},{2,1},{3,2},{4,3},{5,4},{6,5},{7,6},{8,7},{9,8},{10,9},{11,1... | collective-permute-start | bytes 49160 | tf_op jit(solution)/shard_map/ppermute | solution.py:21
  253.4 11.4 %copy-start.11 = (f32[32,128,128]{2,0,1:T(8,128)S(1)}, f32[32,128,128]{2,0,1:T(8,128)}, u32[]{:S(2)}) copy-start(f32[32,128,128]{2,0,1:T(8,128)} %copy-done.10) | copy-start | bytes 6291460
  253.4 11.4 %copy-start.21 = (f32[32,128,1]{2,0,1:T(8,128)S(1)}, f32[32,128,1]{2,0,1:T(8,128)}, u32[]{:S(2)}) copy-start(f32[32,128,1]{2,0,1:T(8,128)} %copy.53) | copy-start | bytes 49156
  253.4 11.4 %copy-start.29 = (f32[32,128,1]{2,0,1:T(8,128)S(1)}, f32[32,128,1]{2,0,1:T(8,128)}, u32[]{:S(2)}) copy-start(f32[32,128,1]{2,0,1:T(8,128)} %copy.54) | copy-start | bytes 49156
  254.5 6.1 %collective-permute-start.26 = (f32[32,1,130]{2,0,1:T(8,128)S(1)}, f32[32,1,130]{2,0,1:T(8,128)S(1)}, u32[]{:S(2)}, u32[]{:S(2)}) collective-permute-start(f32[32,1,130]{2,0,1:T(8,128)S(1)} %get-tuple-element.10), channel_id=1, source_target_pairs={{0,16},{16,32},{32,48},{48,64},{64,80},{80,96},{96,112},{1,17},{17... | collective-permute-start | bytes 49928 | tf_op jit(solution)/shard_map/ppermute | solution.py:19
  258.8 6.0 %collective-permute-start.27 = (f32[32,1,130]{2,0,1:T(8,128)S(1)}, f32[32,1,130]{2,0,1:T(8,128)S(1)}, u32[]{:S(2)}, u32[]{:S(2)}) collective-permute-start(f32[32,1,130]{2,0,1:T(8,128)S(1)} %get-tuple-element.11), channel_id=1, source_target_pairs={{16,0},{32,16},{48,32},{64,48},{80,64},{96,80},{112,96},{17,1},{33... | collective-permute-start | bytes 49928 | tf_op jit(solution)/shard_map/ppermute | solution.py:21
  274.3 7.4 %collective-permute-start.28 = (f32[32,128,1]{1,0,2:T(8,128)S(1)}, f32[32,128,1]{1,0,2:T(8,128)S(1)}, u32[]{:S(2)}, u32[]{:S(2)}) collective-permute-start(f32[32,128,1]{1,0,2:T(8,128)S(1)} %copy.55), channel_id=1, source_target_pairs={{0,1},{1,2},{2,3},{3,4},{4,5},{5,6},{6,7},{7,8},{8,9},{9,10},{10,1... | collective-permute-start | bytes 49160 | tf_op jit(solution)/shard_map/ppermute | solution.py:19
  275.7 11.8 %copy-start.9 = (f32[32,128,128]{2,0,1:T(8,128)S(1)}, f32[32,128,128]{2,0,1:T(8,128)}, u32[]{:S(2)}) copy-start(f32[32,128,128]{2,0,1:T(8,128)} %copy-done.8) | copy-start | bytes 6291460
  275.7 8.9 %collective-permute-start.29 = (f32[32,128,1]{1,0,2:T(8,128)S(1)}, f32[32,128,1]{1,0,2:T(8,128)S(1)}, u32[]{:S(2)}, u32[]{:S(2)}) collective-permute-start(f32[32,128,1]{1,0,2:T(8,128)S(1)} %copy.56), channel_id=1, source_target_pairs={{1,0},{2,1},{3,2},{4,3},{5,4},{6,5},{7,6},{8,7},{9,8},{10,9},{11,1... | collective-permute-start | bytes 49160 | tf_op jit(solution)/shard_map/ppermute | solution.py:21
  287.5 10.8 %copy-start.22 = (f32[32,128,1]{2,0,1:T(8,128)S(1)}, f32[32,128,1]{2,0,1:T(8,128)}, u32[]{:S(2)}) copy-start(f32[32,128,1]{2,0,1:T(8,128)} %copy.57) | copy-start | bytes 49156
  287.5 10.8 %copy-start.30 = (f32[32,128,1]{2,0,1:T(8,128)S(1)}, f32[32,128,1]{2,0,1:T(8,128)}, u32[]{:S(2)}) copy-start(f32[32,128,1]{2,0,1:T(8,128)} %copy.58) | copy-start | bytes 49156
  288.5 6.2 %collective-permute-start.30 = (f32[32,1,130]{2,0,1:T(8,128)S(1)}, f32[32,1,130]{2,0,1:T(8,128)S(1)}, u32[]{:S(2)}, u32[]{:S(2)}) collective-permute-start(f32[32,1,130]{2,0,1:T(8,128)S(1)} %get-tuple-element.8), channel_id=1, source_target_pairs={{0,16},{16,32},{32,48},{48,64},{64,80},{80,96},{96,112},{1,17},{17... | collective-permute-start | bytes 49928 | tf_op jit(solution)/shard_map/ppermute | solution.py:19
  293.1 7.7 %copy-start.12 = (f32[32,128,128]{2,0,1:T(8,128)S(1)}, f32[32,128,128]{2,0,1:T(8,128)}, u32[]{:S(2)}) copy-start(f32[32,128,128]{2,0,1:T(8,128)} %copy-done.10) | copy-start | bytes 6291460
  293.1 5.2 %collective-permute-start.31 = (f32[32,1,130]{2,0,1:T(8,128)S(1)}, f32[32,1,130]{2,0,1:T(8,128)S(1)}, u32[]{:S(2)}, u32[]{:S(2)}) collective-permute-start(f32[32,1,130]{2,0,1:T(8,128)S(1)} %get-tuple-element.9), channel_id=1, source_target_pairs={{16,0},{32,16},{48,32},{64,48},{80,64},{96,80},{112,96},{17,1},{33... | collective-permute-start | bytes 49928 | tf_op jit(solution)/shard_map/ppermute | solution.py:21
  308.5 9.3 %collective-permute-start.32 = (f32[32,128,1]{1,0,2:T(8,128)S(1)}, f32[32,128,1]{1,0,2:T(8,128)S(1)}, u32[]{:S(2)}, u32[]{:S(2)}) collective-permute-start(f32[32,128,1]{1,0,2:T(8,128)S(1)} %copy.59), channel_id=1, source_target_pairs={{0,1},{1,2},{2,3},{3,4},{4,5},{5,6},{6,7},{7,8},{8,9},{9,10},{10,1... | collective-permute-start | bytes 49160 | tf_op jit(solution)/shard_map/ppermute | solution.py:19
  311.2 9.5 %collective-permute-start.33 = (f32[32,128,1]{1,0,2:T(8,128)S(1)}, f32[32,128,1]{1,0,2:T(8,128)S(1)}, u32[]{:S(2)}, u32[]{:S(2)}) collective-permute-start(f32[32,128,1]{1,0,2:T(8,128)S(1)} %copy.60), channel_id=1, source_target_pairs={{1,0},{2,1},{3,2},{4,3},{5,4},{6,5},{7,6},{8,7},{9,8},{10,9},{11,1... | collective-permute-start | bytes 49160 | tf_op jit(solution)/shard_map/ppermute | solution.py:21
  323.6 9.7 %copy-start.14 = (f32[32,128,128]{2,0,1:T(8,128)S(1)}, f32[32,128,128]{2,0,1:T(8,128)}, u32[]{:S(2)}) copy-start(f32[32,128,128]{2,0,1:T(8,128)} %copy-done.13) | copy-start | bytes 6291460
  323.6 9.7 %copy-start.16 = (f32[32,128,1]{2,0,1:T(8,128)S(1)}, f32[32,128,1]{2,0,1:T(8,128)}, u32[]{:S(2)}) copy-start(f32[32,128,1]{2,0,1:T(8,128)} %copy.61) | copy-start | bytes 49156
  323.6 9.7 %copy-start.24 = (f32[32,128,1]{2,0,1:T(8,128)S(1)}, f32[32,128,1]{2,0,1:T(8,128)}, u32[]{:S(2)}) copy-start(f32[32,128,1]{2,0,1:T(8,128)} %copy.62) | copy-start | bytes 49156
  324.6 5.4 %collective-permute-start.34 = (f32[32,1,130]{2,0,1:T(8,128)S(1)}, f32[32,1,130]{2,0,1:T(8,128)S(1)}, u32[]{:S(2)}, u32[]{:S(2)}) collective-permute-start(f32[32,1,130]{2,0,1:T(8,128)S(1)} %get-tuple-element.6), channel_id=1, source_target_pairs={{0,16},{16,32},{32,48},{48,64},{64,80},{80,96},{96,112},{1,17},{17... | collective-permute-start | bytes 49928 | tf_op jit(solution)/shard_map/ppermute | solution.py:19
  328.5 4.8 %collective-permute-start.35 = (f32[32,1,130]{2,0,1:T(8,128)S(1)}, f32[32,1,130]{2,0,1:T(8,128)S(1)}, u32[]{:S(2)}, u32[]{:S(2)}) collective-permute-start(f32[32,1,130]{2,0,1:T(8,128)S(1)} %get-tuple-element.7), channel_id=1, source_target_pairs={{16,0},{32,16},{48,32},{64,48},{80,64},{96,80},{112,96},{17,1},{33... | collective-permute-start | bytes 49928 | tf_op jit(solution)/shard_map/ppermute | solution.py:21
  (12 other events, 34.1 us)
Sparse Core Ops, SparseCore 0:
  197.9 213.0 all-gather.2
